TPU v7x, 32 devices: a whole 2x2x4 slice. The times are simulated.
32 devices in a mesh: frame: 8 (over z, y), row: 4 (over x, core).
Axes of the slice: x: 2, y: 2, z: 4, core: 2. Of those that a mesh axis runs over, the one named last changes fastest.
Arguments:
- features: bfloat16 [16, 64, 64, 640], P('frame', 'row'), may hold values from -6 to 6
- time_weight: bfloat16 [3, 640, 640], replicated, may hold values from -0.125 to 0.125
- time_bias: float32 [640], replicated, may hold values from -3 to 3
- down_weight: bfloat16 [3, 3, 640, 1280], P(None, None, None, 'frame'), may hold values from -0.078125 to 0.078125
- down_bias: float32 [1280], replicated, may hold values from -3 to 3
- norm_gain: float32 [1280], replicated, may hold values from 0.1 to 1.9
- w_query: bfloat16 [1280, 1280], replicated, may hold values from -4 to 4
- w_key: bfloat16 [1280, 1280], replicated, may hold values from -4 to 4
- w_value: bfloat16 [1280, 1280], replicated, may hold values from -0.15625 to 0.15625
- w_out: bfloat16 [1280, 1280], replicated, may hold values from -0.15625 to 0.15625
- out_bias: float32 [1280], replicated, may hold values from -3 to 3
Outputs:
- result: bfloat16 [16, 32, 32, 1280], P('frame', 'row')
All inputs are finite; a program needn't handle non-finite values.
Results may differ from a plain program's by a relative error of at most 0.0085.
Values may be sent and summed in bfloat16 or wider, within the bound.
No kernel may reach another device: no remote copies, remote signals or barrier semaphores. Data moves between devices by JAX's collectives and lax.ppermute only.
A program may use at most 192 MiB of HBM per device.

v0:
```python
import jax
import jax.numpy as jnp
from jax import lax
from jax.sharding import PartitionSpec as P

HEADS = 16


def padded(block, sides, width):
    for axis, dim in sides:
        count = lax.axis_size(axis)
        forward = [(i, i + 1) for i in range(count - 1)]
        backward = [(target, source) for source, target in forward]
        low = lax.ppermute(
            lax.slice_in_dim(block, block.shape[dim] - width, None, axis=dim), axis, forward
        )
        high = lax.ppermute(lax.slice_in_dim(block, 0, width, axis=dim), axis, backward)
        block = jnp.concatenate([low, block, high], axis=dim)
    return block


def passed_along(value, axis, steps):
    count = lax.axis_size(axis)
    leading, last = (max(0, -steps), min(count, count - steps))
    return lax.ppermute(value, axis, [(source, source + steps) for source in range(leading, last)])


def layer_norm(tokens, norm_gain):
    values = tokens.astype(jnp.float32)
    middle_tap = values - jnp.mean(values, axis=-1, keepdims=True)
    spread = jnp.mean(middle_tap * middle_tap, axis=-1, keepdims=True)
    return (middle_tap * lax.rsqrt(spread + 1e-05) * norm_gain).astype(jnp.bfloat16)


def project(normed, weight):
    return jnp.einsum("fnc,cd->fnd", normed, weight, preferred_element_type=jnp.float32).astype(
        jnp.bfloat16
    )


def attend_frames(query_rows, key_rows, value_rows, heads):
    frames, pixels, channels = query_rows.shape
    head_width = channels // heads
    query_heads = query_rows.reshape(frames, pixels, heads, head_width)
    key_heads = key_rows.reshape(frames, pixels, heads, head_width)
    value_heads = value_rows.reshape(frames, pixels, heads, head_width)
    scores = jnp.einsum(
        "fnhd,gnhd->nhfg", query_heads, key_heads, preferred_element_type=jnp.float32
    ) * head_width ** (-0.5)
    weights = jax.nn.softmax(scores, axis=-1).astype(jnp.bfloat16)
    attended = jnp.einsum(
        "nhfg,gnhd->fnhd", weights, value_heads, preferred_element_type=jnp.float32
    )
    return attended.astype(jnp.bfloat16).reshape(frames, pixels, channels)


def shift_columns(values):
    zeros = jnp.zeros(values[:, :, :1].shape, values.dtype)
    return jnp.concatenate([zeros, values[:, :, :-1]], axis=2)


def on_device(
    features,
    time_weight,
    time_bias,
    down_weight,
    down_bias,
    norm_gain,
    w_query,
    w_key,
    w_value,
    w_out,
    out_bias,
):
    frames_here, rows_here, columns, channels = features.shape
    padded_input = padded(features, (("frame", 0),), 1)
    summed = features.astype(jnp.float32) + time_bias
    for tap in range(3):
        summed = summed + jnp.dot(
            padded_input[tap : tap + frames_here],
            time_weight[tap],
            preferred_element_type=jnp.float32,
        )
    hidden_state = summed.astype(jnp.bfloat16)
    above_row = passed_along(hidden_state[:, -1:], "row", 1)
    half_rows = rows_here // 2
    half_cols = columns // 2
    planes = hidden_state.reshape(frames_here, half_rows, 2, half_cols, 2, channels)
    above_planes = above_row.reshape(frames_here, 1, half_cols, 2, channels)
    row_parity = (1, 0, 1)
    col_parity = (1, 0, 1)
    local_columns = down_weight.reshape(9 * channels, down_weight.shape[3])
    weight_piece = lax.all_gather(local_columns, "frame", axis=1, tiled=True)
    width = weight_piece.shape[1]
    kernel = weight_piece.reshape(3, 3, channels, width)
    total = jnp.zeros((frames_here, half_rows, half_cols, width), jnp.float32) + down_bias
    for row_shifted in (True, False):
        for col_shifted in (True, False):
            inner = jnp.zeros((frames_here, half_rows, half_cols, width), jnp.float32)
            upper = jnp.zeros((frames_here, 1, half_cols, width), jnp.float32)
            for row_tap in range(3):
                if (row_tap == 0) != row_shifted:
                    continue
                for col_tap in range(3):
                    if (col_tap == 0) != col_shifted:
                        continue
                    tap_kernel = kernel[row_tap, col_tap]
                    source = planes[:, :, row_parity[row_tap], :, col_parity[col_tap]]
                    inner = inner + jnp.dot(source, tap_kernel, preferred_element_type=jnp.float32)
                    if row_shifted:
                        upper = upper + jnp.dot(
                            above_planes[:, :, :, col_parity[col_tap]],
                            tap_kernel,
                            preferred_element_type=jnp.float32,
                        )
            if col_shifted:
                inner = shift_columns(inner)
                upper = shift_columns(upper)
            if row_shifted:
                inner = jnp.concatenate([upper, inner[:, :-1]], axis=1)
            total = total + inner
    coarse_grid = total.astype(jnp.bfloat16).reshape(frames_here * half_rows * half_cols, width)
    model_width = coarse_grid.shape[1]
    groups = lax.axis_size("frame")
    pixels_here = half_rows * half_cols
    tokens = coarse_grid.reshape(frames_here, groups, pixels_here // groups, model_width)
    moved = lax.all_to_all(tokens, "frame", split_axis=1, concat_axis=0, tiled=True)
    all_frames = moved.shape[0]
    flat = moved.reshape(all_frames, moved.shape[2], model_width)
    normed = layer_norm(flat, norm_gain)
    attended = attend_frames(
        project(normed, w_query), project(normed, w_key), project(normed, w_value), HEADS
    )
    gathered = attended.reshape(moved.shape)
    returned = lax.all_to_all(gathered, "frame", split_axis=0, concat_axis=1, tiled=True)
    returned = returned.reshape(frames_here, pixels_here, model_width)
    output = jnp.einsum("fnc,cd->fnd", returned, w_out, preferred_element_type=jnp.float32)
    residual = coarse_grid.reshape(frames_here, pixels_here, model_width).astype(jnp.float32)
    result = (residual + output + out_bias).astype(jnp.bfloat16)
    return result.reshape(frames_here, half_rows, half_cols, model_width)


def solution(mesh):
    return jax.shard_map(
        on_device,
        mesh=mesh,
        in_specs=(
            P("frame", "row", None, None),
            P(),
            P(),
            P(None, None, None, "frame"),
            P(),
            P(),
            P(),
            P(),
            P(),
            P(),
            P(),
        ),
        out_specs=P("frame", "row", None, None),
        check_vma=False,
    )
```

profile of v0, /device:TPU:0, one launch (start us, length us, event | category | flops | bytes accessed | tf_op | source)
XLA Modules:
  0.0 427.1 jit_solution(17917234597291021083)
XLA Ops:
  6.5 4.4 %copy.41 = bf16[3,3,640,160]{2,1,0,3:T(4,128)(2,1)} copy(bf16[3,3,640,160]{2,3,1,0:T(8,128)(2,1)} %param.14) | data formatting | bytes 3686400 | tf_op args[3]
  10.9 5.1 %reshape.89 = bf16[5760,160]{0,1:T(8,128)(2,1)} reshape(bf16[3,3,640,160]{2,1,0,3:T(4,128)(2,1)} %copy.41) | data formatting | bytes 3686400 | tf_op jit(solution)/shard_map/reshape | solution.py:92
  16.1 2.1 fusion.86
  18.2 5.1 %collective-permute-start = (bf16[1,16,64,640]{3,2,1,0:T(8,128)(2,1)S(1)}, bf16[1,16,64,640]{3,2,1,0:T(8,128)(2,1)S(1)}, u32[]{:S(2)}, u32[]{:S(2)}) collective-permute-start(bf16[1,16,64,640]{3,2,1,0:T(8,128)(2,1)S(1)} %get-tuple-element.10), channel_id=1, source_target_pairs={{0,4},{4,8},{8,12},{12,16},{16,20},{20,24},{24,28},{1,5},{5,9},{9,... | collective-permute-start | bytes 3932168 | tf_op jit(solution)/shard_map/ppermute | solution.py:14
  24.6 2.5 fusion.73
  27.2 71.9 %collective-permute-done = bf16[1,16,64,640]{3,2,1,0:T(8,128)(2,1)S(1)} collective-permute-done((bf16[1,16,64,640]{3,2,1,0:T(8,128)(2,1)S(1)}, bf16[1,16,64,640]{3,2,1,0:T(8,128)(2,1)S(1)}, u32[]{:S(2)}, u32[]{:S(2)}) %collective-permute-start) | collective-permute-done | bytes 1310752 | tf_op jit(solution)/shard_map/ppermute | solution.py:14
  99.1 2.5 fusion.1
  101.6 4.0 add_convert_fusion
  105.6 6.5 %reshape.91 = bf16[2,8,2,32,2,640]{5,4,3,2,1,0:T(2,128)(2,1)} reshape(bf16[2,16,64,640]{3,2,1,0:T(8,128)(2,1)} %add_convert_fusion) | data formatting | bytes 5242880 | tf_op jit(solution)/shard_map/reshape | solution.py:88
  113.0 2.1 collective-permute-start.2
  115.1 7.7 %fusion.85 = (bf16[2,8,1,32,1,640]{5,4,3,2,1,0:T(2,128)(2,1)S(1)}, bf16[2,8,1,32,1,640]{5,4,3,2,1,0:T(2,128)(2,1)}, bf16[2,8,1,32,1,640]{5,4,3,2,1,0:T(2,128)(2,1)}, bf16[2,8,1,32,1,640]{5,4,3,2,1,0:T(2,128)(2,1)}) fusion(bf16[2,8,2,32,2,640]{5,4,3,2,1,0:T(2,128)(2,1)} %reshape.91), kind=kLoop, calls=%fused_computation.104 | loop fusion | bytes 5242880 | tf_op jit(solution)/shard_map/slice | solution.py:108
  125.6 128.1 %all-gather.2.cloned.1.call-done = bf16[5760,1280]{0,1:T(8,128)(2,1)} async-done(((bf16[5760,160]{0,1:T(8,128)(2,1)}), bf16[5760,1280]{0,1:T(8,128)(2,1)}) %all-gather.2.cloned.1.call-update) | async-done | bytes 14745616 | tf_op jit(solution)/shard_map/all_gather | solution.py:93
  253.7 18.8 %copy.42 = bf16[5760,1280]{1,0:T(8,128)(2,1)} copy(bf16[5760,1280]{0,1:T(8,128)(2,1)} %all-gather.2.cloned.1.call-done) | data formatting | bytes 29491200 | tf_op jit(solution)/shard_map/all_gather | solution.py:93
  272.5 3.0 fusion.61
  275.5 4.9 %fusion.54 = f32[2,8,32,1280]{3,2,1,0:T(8,128)} fusion(bf16[2,8,32,640]{3,2,1,0:T(8,128)(2,1)S(1)} %bitcast.210, bf16[3,3,640,1280]{3,2,1,0:T(8,128)(2,1)} %bitcast.195), kind=kOutput, calls=%fused_computation.66 | convolution fusion | flops 838860800 | bytes 4915200 | tf_op jit(solution)/shard_map/dot_general | solution.py:109
  283.9 2.7 fusion.52
  290.5 2.7 fusion.56
  295.2 3.0 pad_slice_fusion
  299.7 34.3 %all_to_all.24 = bf16[2,8,32,1280]{3,2,0,1:T(8,128)(2,1)S(1)} all-to-all(bf16[2,8,32,1280]{3,2,0,1:T(8,128)(2,1)S(1)} %copy.49), channel_id=1, replica_groups=mesh['frame'=8,'row'=4] {'frame'}, dimensions={1} | all-to-all | bytes 2621440 | tf_op jit(solution)/shard_map/all_to_all | solution.py:127
  336.4 2.9 fusion.27
  339.3 5.0 %reshape.95 = bf16[16,32,16,80]{3,2,1,0:T(8,128)(2,1)} reshape(bf16[16,32,1280]{2,1,0:T(8,128)(2,1)} %fusion.27) | data formatting | bytes 2621440 | tf_op jit(solution)/shard_map/reshape | solution.py:45
  344.3 5.2 %fusion.24 = bf16[16,32,1280]{2,1,0:T(8,128)(2,1)} fusion(bf16[16,32,1280]{2,1,0:T(8,128)(2,1)} %copy-done.9, bf16[1280,1280]{1,0:T(8,128)(2,1)} %param.17), kind=kOutput, calls=%fused_computation.28 | convolution fusion | flops 1678376960 | bytes 5898240 | tf_op jit(solution)/shard_map/fnc,cd->fnd/dot_general | solution.py:36
  349.6 5.2 %reshape.94 = bf16[16,32,16,80]{3,2,1,0:T(8,128)(2,1)} reshape(bf16[16,32,1280]{2,1,0:T(8,128)(2,1)} %fusion.24) | data formatting | bytes 2621440 | tf_op jit(solution)/shard_map/reshape | solution.py:44
  354.8 4.8 %fusion.44 = f32[32,16,16,16]{2,3,1,0:T(8,128)S(1)} fusion(bf16[16,32,16,80]{3,2,1,0:T(8,128)(2,1)} %reshape.95, bf16[16,32,16,80]{3,2,1,0:T(8,128)(2,1)} %reshape.94), kind=kOutput, calls=%fused_computation.51 | convolution fusion | flops 20971520 | bytes 3145728 | tf_op jit(solution)/shard_map/fnhd,gnhd->nhfg/dot_general | solution.py:47
  359.6 3.5 fusion.88
  363.1 2.9 fusion.21
  366.0 5.0 %reshape.93 = bf16[16,32,16,80]{3,2,1,0:T(8,128)(2,1)} reshape(bf16[16,32,1280]{2,1,0:T(8,128)(2,1)} %fusion.21) | data formatting | bytes 2621440 | tf_op jit(solution)/shard_map/reshape | solution.py:46
  371.0 4.4 %convert_bitcast_fusion = bf16[16,32,16,80]{3,0,2,1:T(8,128)(2,1)S(1)} fusion(f32[32,16,16,16]{2,3,1,0:T(8,128)} %get-tuple-element.14, f32[32,16,16]{2,1,0:T(8,128)S(1)} %get-tuple-element.13, bf16[16,32,16,80]{3,2,1,0:T(8,128)(2,1)} %reshape.93), kind=kOutput, calls=%fused_computation.54 | convolution fusion | flops 21889024 | bytes 3178496 | tf_op jit(solution)/shard_map/nhfg,gnhd->fnhd/dot_general | solution.py:51
  375.4 1.9 copy.59
  377.3 4.5 %reshape_reshape.4 = bf16[16,1,32,1280]{3,2,0,1:T(8,128)(2,1)} reshape(bf16[16,32,16,80]{3,2,1,0:T(8,128)(2,1)} %copy.59) | data formatting | bytes 2621440 | tf_op jit(solution)/shard_map/reshape;reshape | solution.py:134
  381.9 34.9 %all_to_all.25 = bf16[16,1,32,1280]{3,2,1,0:T(8,128)(2,1)S(1)} all-to-all(bf16[16,1,32,1280]{3,2,1,0:T(8,128)(2,1)} %bitcast.206), channel_id=1, replica_groups=mesh['frame'=8,'row'=4] {'frame'}, dimensions={0} | all-to-all | bytes 2621440 | tf_op jit(solution)/shard_map/all_to_all | solution.py:135
  416.9 2.9 fusion.30
  (68 shorter events, 18.4 us)
Async XLA Ops:
  6.5 329.9 %copy-start = (bf16[1280,1280]{1,0:T(8,128)(2,1)S(1)}, bf16[1280,1280]{1,0:T(8,128)(2,1)}, u32[]{:S(2)}) copy-start(bf16[1280,1280]{1,0:T(8,128)(2,1)} %param.18) | copy-start | bytes 9830404
  6.5 247.2 %all-gather.2.cloned.1.call-start = ((), (), s32[]{:S(2)}) async-start(), calls=%async_computation.2 | async-start | bytes 16588800 | tf_op jit(solution)/shard_map/all_gather | solution.py:93
  16.1 8.5 %copy-start.2 = (bf16[2,16,64,640]{3,2,1,0:T(8,128)(2,1)S(1)}, bf16[2,16,64,640]{3,2,1,0:T(8,128)(2,1)}, u32[]{:S(2)}) copy-start(bf16[2,16,64,640]{3,2,1,0:T(8,128)(2,1)} %param.11) | copy-start | bytes 7864324
  16.1 8.5 %copy-start.13 = (bf16[3,640,640]{2,1,0:T(8,128)(2,1)S(1)}, bf16[3,640,640]{2,1,0:T(8,128)(2,1)}, u32[]{:S(2)}) copy-start(bf16[3,640,640]{2,1,0:T(8,128)(2,1)} %param.12) | copy-start | bytes 7372804
  18.2 80.9 %collective-permute-start = (bf16[1,16,64,640]{3,2,1,0:T(8,128)(2,1)S(1)}, bf16[1,16,64,640]{3,2,1,0:T(8,128)(2,1)S(1)}, u32[]{:S(2)}, u32[]{:S(2)}) collective-permute-start(bf16[1,16,64,640]{3,2,1,0:T(8,128)(2,1)S(1)} %get-tuple-element.10), channel_id=1, source_target_pairs={{0,4},{4,8},{8,12},{12,16},{16,20},{20,24},{24,28},{1,5},{5,9},{9,... | collective-permute-start | bytes 3932168 | tf_op jit(solution)/shard_map/ppermute | solution.py:14
  23.3 78.3 %collective-permute-start.1 = (bf16[1,16,64,640]{3,2,1,0:T(8,128)(2,1)S(1)}, bf16[1,16,64,640]{3,2,1,0:T(8,128)(2,1)S(1)}, u32[]{:S(2)}, u32[]{:S(2)}) collective-permute-start(bf16[1,16,64,640]{3,2,1,0:T(8,128)(2,1)S(1)} %get-tuple-element.9), channel_id=1, source_target_pairs={{4,0},{8,4},{12,8},{16,12},{20,16},{24,20},{28,24},{5,1},{9,5},{13... | collective-permute-start | bytes 3932168 | tf_op jit(solution)/shard_map/ppermute | solution.py:17
  27.2 74.5 %copy-start.15 = (f32[640]{0:T(1024)S(1)}, f32[640]{0:T(1024)}, u32[]{:S(2)}) copy-start(f32[640]{0:T(1024)} %param.13) | copy-start | bytes 7684
  113.0 10.7 %collective-permute-start.2 = (bf16[2,1,64,640]{3,2,1,0:T(8,128)(2,1)S(1)}, bf16[2,1,64,640]{3,2,1,0:T(8,128)(2,1)}, u32[]{:S(2)}, u32[]{:S(2)}) collective-permute-start(bf16[2,1,64,640]{3,2,1,0:T(8,128)(2,1)S(1)} %slice.121), channel_id=1, source_target_pairs={{0,1},{1,2},{2,3},{4,5},{5,6},{6,7},{8,9},{9,10},{10,11},{12,13},{... | collective-permute-start | bytes 491528 | tf_op jit(solution)/shard_map/ppermute | solution.py:25
  253.7 26.6 %copy-start.11 = (bf16[2,1,32,1,640]{4,3,2,0,1:T(2,128)(2,1)S(1)}, bf16[2,1,32,1,640]{4,3,2,0,1:T(2,128)(2,1)}, u32[]{:S(2)}) copy-start(bf16[2,1,32,1,640]{4,3,2,0,1:T(2,128)(2,1)} %get-tuple-element.12) | copy-start | bytes 245764
  272.5 3.0 copy-start.7
  272.5 14.2 %copy-start.1 = (bf16[5760,1280]{1,0:T(8,128)(2,1)S(1)}, bf16[5760,1280]{1,0:T(8,128)(2,1)}, u32[]{:S(2)}) copy-start(bf16[5760,1280]{1,0:T(8,128)(2,1)} %copy.42) | copy-start | bytes 44236804
  283.9 2.8 copy-start.8
  286.7 1.3 copy-start.6
  289.2 1.3 copy-start.5
  293.2 1.2 copy-start.12
  295.2 3.0 copy-start.14
  299.6 34.4 %copy-start.3 = (bf16[2,8,32,1280]{3,2,1,0:T(8,128)(2,1)}, bf16[2,8,32,1280]{3,2,1,0:T(8,128)(2,1)S(1)}, u32[]{:S(2)}) copy-start(bf16[2,8,32,1280]{3,2,1,0:T(8,128)(2,1)S(1)} %fusion.33) | copy-start | bytes 3932164
  299.7 35.1 %copy-start.16 = (f32[1280]{0:T(1024)S(1)}, f32[1280]{0:T(1024)}, u32[]{:S(2)}) copy-start(f32[1280]{0:T(1024)} %param.16) | copy-start | bytes 15364
  335.3 1.1 copy-start.9
  359.6 3.5 copy-start.10
  359.6 3.5 copy-start.17
  381.9 35.0 %copy-start.4 = (bf16[2,8,32,1280]{3,2,1,0:T(8,128)(2,1)S(1)}, bf16[2,8,32,1280]{3,2,1,0:T(8,128)(2,1)}, u32[]{:S(2)}) copy-start(bf16[2,8,32,1280]{3,2,1,0:T(8,128)(2,1)} %copy-done.3) | copy-start | bytes 3932164
  381.9 35.1 %copy-start.18 = (bf16[1280,1280]{1,0:T(8,128)(2,1)S(1)}, bf16[1280,1280]{1,0:T(8,128)(2,1)}, u32[]{:S(2)}) copy-start(bf16[1280,1280]{1,0:T(8,128)(2,1)} %param.20) | copy-start | bytes 9830404
  381.9 35.1 %copy-start.19 = (f32[1280]{0:T(1024)S(1)}, f32[1280]{0:T(1024)}, u32[]{:S(2)}) copy-start(f32[1280]{0:T(1024)} %param.21) | copy-start | bytes 15364
Sparse Core Ops, SparseCore 0:
  16.2 237.4 all-gather.1
where the time goes:
time: 436 us; the launch traced here: 427 us
  waiting for transfers between devices  200 us (46%)
  local copies, waits for them, and re-layouts  71.5 us (16%)
  blocking collectives  69.2 us (16%)
  matrix products  55.6 us (13%)
  between operations  14.2 us (3%)
  starting transfers between devices  8.51 us (2%)
  other arithmetic  8.1 us (2%)
    all_gather x1, waiting for transfers between devices, on_device(): weight_piece = lax.all_gather(local_columns, 'frame', axis=1, tiled=True)  128 us
    ppermute x1, waiting for transfers between devices, padded(): lax.ppermute(lax.slice_in_dim(block, block.shape[dim] - width, None, axis...  71.9 us
    all_to_all x1, blocking collectives, on_device(): lax.all_to_all(gathered, 'frame', split_axis=0, concat_axis=1, tiled=True)  34.9 us
    all_to_all x1, blocking collectives, on_device(): lax.all_to_all(tokens, 'frame', split_axis=1, concat_axis=0, tiled=True)  34.3 us
    dot_general x9, matrix products, on_device(): jnp.dot(source, tap_kernel, preferred_element_type=jnp.float32)  19.4 us
    all_gather x1, local copies, waits for them, and re-layouts, on_device(): weight_piece = lax.all_gather(local_columns, 'frame', axis=1, tiled=True)  18.8 us
    dot_general x3, matrix products, project(): jnp.einsum('fnc,cd->fnd', normed, weight, preferred_element_type=jnp.floa...  11.1 us
    dot_general x3, matrix products, on_device(): jnp.dot(padded_input[tap:tap + frames_here], time_weight[tap], preferred_...  9.04 us
  transfers between devices with their start and end apart: 4, of which 2 were waited for; matrix products, arithmetic and copies ran while one was open for 7% of the time, Pallas kernels for 0%

commit v1 on v0

v1 whole, which is shorter than its diff:
```python
import functools

import jax
import jax.numpy as jnp
from jax import lax
from jax.experimental import pallas as pl
from jax.experimental.pallas import tpu as pltpu
from jax.sharding import PartitionSpec as P

HEADS = 16
LANES = 128
MASKED = -3.0e38


def passed_along(value, axis, steps):
    count = lax.axis_size(axis)
    leading, last = (max(0, -steps), min(count, count - steps))
    return lax.ppermute(value, axis, [(source, source + steps) for source in range(leading, last)])


def weight_part_kernel(part, index_ref, weight_ref, out_ref):
    columns = weight_ref.shape[1]
    rows = lax.broadcasted_iota(jnp.int32, (part, columns), 0) + index_ref[0] * part
    chosen = rows == lax.broadcasted_iota(jnp.int32, (part, columns), 1)
    out_ref[...] = lax.dot_general(
        chosen.astype(jnp.bfloat16),
        weight_ref[...],
        (((1,), (1,)), ((), ())),
        preferred_element_type=jnp.float32,
    ).astype(jnp.bfloat16)


def weight_part(local_columns, parts, index):
    depth, columns = local_columns.shape
    part = columns // parts
    step = depth // 3
    return pl.pallas_call(
        functools.partial(weight_part_kernel, part),
        out_shape=jax.ShapeDtypeStruct((part, depth), jnp.bfloat16),
        grid=(3,),
        in_specs=[
            pl.BlockSpec(memory_space=pltpu.SMEM),
            pl.BlockSpec((step, columns), lambda k: (k, 0)),
        ],
        out_specs=pl.BlockSpec((part, step), lambda k: (0, k)),
        cost_estimate=pl.CostEstimate(
            flops=2 * part * columns * depth, bytes_accessed=2 * depth * (columns + part), transcendentals=0
        ),
    )(index.reshape(1), local_columns)


def temporal_kernel(before_ref, centre_ref, after_ref, weight_ref, bias_ref, out_ref, held):
    rows, columns, channels = centre_ref.shape[1:]
    count = rows * columns
    centre = centre_ref[...].reshape(count, channels)
    total = centre.astype(jnp.float32) + bias_ref[...]
    for tap, value in enumerate((before_ref[...], centre_ref[...], after_ref[...])):
        total = total + jnp.dot(
            value.reshape(count, channels), weight_ref[tap], preferred_element_type=jnp.float32
        )
    total = total.astype(jnp.bfloat16).astype(jnp.float32)
    half = columns // 2
    first = lax.broadcasted_iota(jnp.int32, (rows * half, LANES), 0) % half == 0
    for block in range(channels // LANES):
        low = block * LANES
        held[block, 8:, :] = total[:, low : low + LANES]
        moved = held[block, pl.ds(7, rows * half, stride=2), :]
        even = held[block, pl.ds(8, rows * half, stride=2), :]
        odd = held[block, pl.ds(9, rows * half, stride=2), :]
        moved = jnp.where(first, 0.0, moved)
        for place, plane in enumerate((moved, even, odd)):
            start = place * channels + low
            out_ref[:, 0, :, start : start + LANES] = plane.astype(jnp.bfloat16).reshape(rows, half, LANES)


def temporal(before, centre, after, time_weight, time_bias, rows_step):
    frames, rows, columns, channels = centre.shape
    block = (1, rows_step, columns, channels)
    half = columns // 2
    return pl.pallas_call(
        temporal_kernel,
        out_shape=jax.ShapeDtypeStruct((rows, frames, half, 3 * channels), jnp.bfloat16),
        grid=(frames, rows // rows_step),
        in_specs=[
            pl.BlockSpec(block, lambda f, r: (f, r, 0, 0)),
            pl.BlockSpec(block, lambda f, r: (f, r, 0, 0)),
            pl.BlockSpec(block, lambda f, r: (f, r, 0, 0)),
            pl.BlockSpec(time_weight.shape, lambda f, r: (0, 0, 0)),
            pl.BlockSpec((1, channels), lambda f, r: (0, 0)),
        ],
        out_specs=pl.BlockSpec((rows_step, 1, half, 3 * channels), lambda f, r: (r, f, 0, 0)),
        scratch_shapes=[
            pltpu.VMEM((channels // LANES, 8 + rows_step * columns, LANES), jnp.float32)
        ],
        cost_estimate=pl.CostEstimate(
            flops=6 * frames * rows * columns * channels * channels,
            bytes_accessed=9 * frames * rows * columns * channels,
            transcendentals=0,
        ),
    )(before, centre, after, time_weight, time_bias.reshape(1, channels))


def strided_kernel(planes_ref, upper_ref, weight_ref, bias_ref, out_ref, total):
    row_tap = pl.program_id(1)
    half_rows, _, frames, half_cols, width = planes_ref.shape
    count = half_rows * frames * half_cols

    def product(values):
        return lax.dot_general(
            values.reshape(count, width),
            weight_ref[...],
            (((1,), (1,)), ((), ())),
            preferred_element_type=jnp.float32,
        )

    @pl.when(row_tap == 0)
    def _():
        values = jnp.concatenate([upper_ref[...], planes_ref[: half_rows - 1, 1]], axis=0)
        total[...] = product(values) + bias_ref[...]

    @pl.when(row_tap == 1)
    def _():
        total[...] += product(planes_ref[:, 0])

    @pl.when(row_tap == 2)
    def _():
        done = total[...] + product(planes_ref[:, 1])
        out_ref[...] = done.astype(jnp.bfloat16).reshape(out_ref.shape)


def strided(planes, upper, weight, bias, step):
    rows, frames, half_cols, width = planes.shape
    channels = weight.shape[0]
    half_rows = rows // 2
    count = half_rows * frames * half_cols
    return pl.pallas_call(
        strided_kernel,
        out_shape=jax.ShapeDtypeStruct((half_rows, frames, half_cols, channels), jnp.bfloat16),
        grid=(channels // step, 3),
        in_specs=[
            pl.BlockSpec((half_rows, 2, frames, half_cols, width), lambda n, a: (0, 0, 0, 0, 0)),
            pl.BlockSpec((1, frames, half_cols, width), lambda n, a: (0, 0, 0, 0)),
            pl.BlockSpec((step, width), lambda n, a: (n, a)),
            pl.BlockSpec((1, step), lambda n, a: (0, n)),
        ],
        out_specs=pl.BlockSpec((half_rows, frames, half_cols, step), lambda n, a: (0, 0, 0, n)),
        scratch_shapes=[pltpu.VMEM((count, step), jnp.float32)],
        cost_estimate=pl.CostEstimate(
            flops=6 * count * width * channels,
            bytes_accessed=2 * (planes.size + weight.size + count * channels),
            transcendentals=0,
        ),
    )(planes.reshape(half_rows, 2, frames, half_cols, width), upper, weight, bias.reshape(1, channels))


def attention_kernel(
    tokens_ref, gain_ref, bias_ref, wq_hbm, wk_hbm, wv_hbm, wo_hbm, out_ref,
    wq, wk, wv, wo, normed, query, key, value, sems,
):
    copies = []
    for place, (source, target) in enumerate(((wq_hbm, wq), (wk_hbm, wk), (wv_hbm, wv), (wo_hbm, wo))):
        copies.append(pltpu.make_async_copy(source, target, sems.at[place]))
        copies[-1].start()
    frames, pixels, width = tokens_ref.shape
    groups = pixels // 8
    rows = frames * 8
    head_width = width // HEADS
    scale = head_width ** (-0.5)
    for group in range(groups):
        tokens = tokens_ref[:, group * 8 : group * 8 + 8, :].astype(jnp.float32).reshape(rows, width)
        centred = tokens - jnp.mean(tokens, axis=-1, keepdims=True)
        spread = jnp.mean(centred * centred, axis=-1, keepdims=True)
        result = centred * lax.rsqrt(spread + 1e-05) * gain_ref[...]
        normed[group * rows : (group + 1) * rows, :] = result.astype(jnp.bfloat16)
    step = 256
    for place, (weight, target) in enumerate(((wq, query), (wk, key), (wv, value))):
        copies[place].wait()

        @pl.loop(0, width // step)
        def _(n):
            part = pl.ds(pl.multiple_of(n * step, step), step)
            target[:, part] = jnp.dot(
                normed[...], weight[:, part], preferred_element_type=jnp.float32
            ).astype(jnp.bfloat16)

    same = (
        lax.broadcasted_iota(jnp.int32, (rows, rows), 0) % 8
        == lax.broadcasted_iota(jnp.int32, (rows, rows), 1) % 8
    )

    @pl.loop(0, groups)
    def _(group):
        here = pl.ds(pl.multiple_of(group * rows, rows), rows)
        sums = [None] * (width // LANES)
        for head in range(HEADS):
            low = head * head_width // LANES
            high = ((head + 1) * head_width - 1) // LANES + 1
            window = slice(low * LANES, high * LANES)
            lane = lax.broadcasted_iota(jnp.int32, (rows, (high - low) * LANES), 1) + low * LANES
            mine = (lane >= head * head_width) & (lane < (head + 1) * head_width)
            zeros = jnp.zeros((rows, (high - low) * LANES), jnp.bfloat16)
            queries = jnp.where(mine, query[here, window], zeros)
            scores = lax.dot_general(
                queries, key[here, window], (((1,), (1,)), ((), ())), preferred_element_type=jnp.float32
            )
            scores = jnp.where(same, scores * scale, MASKED)
            powers = jnp.exp(scores - jnp.max(scores, axis=-1, keepdims=True))
            weights = powers * (1.0 / jnp.sum(powers, axis=-1, keepdims=True))
            values = jnp.where(mine, value[here, window], zeros)
            part = jnp.dot(weights.astype(jnp.bfloat16), values, preferred_element_type=jnp.float32)
            for block in range(low, high):
                piece = part[:, (block - low) * LANES : (block - low + 1) * LANES]
                sums[block] = piece if sums[block] is None else sums[block] + piece
        for block, total in enumerate(sums):
            normed[here, block * LANES : (block + 1) * LANES] = total.astype(jnp.bfloat16)

    copies[3].wait()

    @pl.loop(0, width // step)
    def _(n):
        part = pl.ds(pl.multiple_of(n * step, step), step)
        output = jnp.dot(normed[...], wo[:, part], preferred_element_type=jnp.float32)
        output = output + bias_ref[:, part]
        for group in range(groups):
            tokens = tokens_ref[:, group * 8 : group * 8 + 8, part].astype(jnp.float32)
            piece = output[group * rows : (group + 1) * rows].reshape(frames, 8, step) + tokens
            out_ref[:, group * 8 : group * 8 + 8, part] = piece.astype(jnp.bfloat16)


def attention(tokens, norm_gain, out_bias, w_query, w_key, w_value, w_out):
    frames, pixels, width = tokens.shape
    count = frames * pixels
    weight = pltpu.VMEM((width, width), jnp.bfloat16)
    rows = pltpu.VMEM((count, width), jnp.bfloat16)
    anywhere = pl.BlockSpec(memory_space=pl.ANY)
    inside = pl.BlockSpec(memory_space=pltpu.VMEM)
    return pl.pallas_call(
        attention_kernel,
        out_shape=jax.ShapeDtypeStruct(tokens.shape, jnp.bfloat16),
        in_specs=[inside, inside, inside, anywhere, anywhere, anywhere, anywhere],
        out_specs=inside,
        scratch_shapes=[weight] * 4 + [rows] * 4 + [pltpu.SemaphoreType.DMA((4,))],
        cost_estimate=pl.CostEstimate(
            flops=8 * count * width * width,
            bytes_accessed=8 * width * width + 4 * count * width,
            transcendentals=count * HEADS * frames * 8,
        ),
    )(
        tokens, norm_gain.reshape(1, width), out_bias.reshape(1, width), w_query, w_key, w_value, w_out
    )


def on_device(
    features,
    time_weight,
    time_bias,
    down_weight,
    down_bias,
    norm_gain,
    w_query,
    w_key,
    w_value,
    w_out,
    out_bias,
):
    frames_here, rows_here, columns, channels = features.shape
    groups = lax.axis_size("frame")
    row_devices = lax.axis_size("row")
    local_columns = down_weight.reshape(9 * channels, down_weight.shape[3])
    part = weight_part(local_columns, row_devices, lax.axis_index("row"))
    weight = lax.all_gather(part, ("frame", "row"), axis=0, tiled=True)
    model_width = weight.shape[0]

    low = passed_along(features[-1:], "frame", 1)
    high = passed_along(features[:1], "frame", -1)
    before = jnp.concatenate([low, features[:-1]], axis=0)
    after = jnp.concatenate([features[1:], high], axis=0)
    planes = temporal(before, features, after, time_weight, time_bias, rows_here // 2)
    upper = passed_along(planes[-1:], "row", 1)
    coarse = strided(planes, upper, weight, down_bias, 256)

    half_rows, half_cols = rows_here // 2, columns // 2
    pixels_here = half_rows * half_cols // groups
    tokens = coarse
    if groups != half_rows:
        tokens = tokens.transpose(1, 0, 2, 3).reshape(frames_here, groups, pixels_here, model_width)
        tokens = tokens.transpose(1, 0, 2, 3)
    moved = lax.all_to_all(tokens, "frame", split_axis=0, concat_axis=0, tiled=True)
    moved = moved.reshape(groups * frames_here, pixels_here, model_width)
    result = attention(moved, norm_gain, out_bias, w_query, w_key, w_value, w_out)
    result = result.reshape(groups, frames_here, pixels_here, model_width)
    returned = lax.all_to_all(result, "frame", split_axis=0, concat_axis=0, tiled=True)
    returned = returned.transpose(1, 0, 2, 3)
    return returned.reshape(frames_here, half_rows, half_cols, model_width)


def solution(mesh):
    return jax.shard_map(
        on_device,
        mesh=mesh,
        in_specs=(
            P("frame", "row", None, None),
            P(),
            P(),
            P(None, None, None, "frame"),
            P(),
            P(),
            P(),
            P(),
            P(),
            P(),
            P(),
        ),
        out_specs=P("frame", "row", None, None),
        check_vma=False,
    )
```

time: 436 us -> 278 us (0.64); the launches traced: 427 us -> 277 us
  Pallas kernels: 0 us -> 60.8 us
  local copies, waits for them, and re-layouts: 71.5 us -> 10.8 us
  waiting for transfers between devices: 200 us -> 140 us
  matrix products: 55.6 us -> 0 us
  blocking collectives: 69.2 us -> 35.2 us
  other arithmetic: 8.1 us -> 3.54 us
    all_gather x1, waiting for transfers between devices: 128 us -> 46.4 us  [on_device(): weight = lax.all_gather(part, ('frame', 'row'), axis=0, tiled=True)]
    ppermute x2 -> x0, waiting for transfers between devices: 71.9 us -> none  [the longest x1 71.9 us: padded(): lax.ppermute(lax.slice_in_dim(block, block.shape[dim] - width, None, axis...]
    ppermute x1 -> x3, waiting for transfers between devices: 0.01 us -> 63.3 us  [passed_along(): lax.ppermute(value, axis, [(source, source + steps) for source in range(l...]
    pallas_call x0 -> x4, Pallas kernels: none -> 60.8 us  [the longest x1 26.6 us: attention(): pl.pallas_call(attention_kernel, out_shape=jax.ShapeDtypeStruct(tokens.sh...]
    dot_general x21 -> x0, matrix products: 55.6 us -> none  [the longest x9 19.4 us: on_device(): jnp.dot(source, tap_kernel, preferred_element_type=jnp.float32)]
    all_to_all x2 -> x1, blocking collectives: 69.2 us -> 35.2 us  [on_device(): lax.all_to_all(result, 'frame', split_axis=0, concat_axis=0, tiled=True)]
    all_to_all x0 -> x1, waiting for transfers between devices: none -> 30.6 us  [on_device(): lax.all_to_all(tokens, 'frame', split_axis=0, concat_axis=0, tiled=True)]
    reshape x6 -> x4, local copies, waits for them, and re-layouts: 27.8 us -> 2.38 us  [the longest x1 0.61 us: strided(): bias.reshape(1, channels)]
  transfers between devices with their start and end apart: 4 -> 5, of which waited for: 2 -> 5; matrix products, arithmetic and copies ran while one was open for 7% -> 3% of each run, Pallas kernels for 0% -> 4%
where the time goes in v1:
time: 278 us; the launch traced here: 277 us
  waiting for transfers between devices  140 us (50%)
  Pallas kernels  60.8 us (22%)
  blocking collectives  35.2 us (13%)
  between operations  13.5 us (5%)
  starting transfers between devices  12.8 us (5%)
  local copies, waits for them, and re-layouts  10.8 us (4%)
  other arithmetic  3.54 us (1%)
    ppermute x3, waiting for transfers between devices, passed_along(): lax.ppermute(value, axis, [(source, source + steps) for source in range(l...  63.3 us
    all_gather x1, waiting for transfers between devices, on_device(): weight = lax.all_gather(part, ('frame', 'row'), axis=0, tiled=True)  46.4 us
    all_to_all x1, blocking collectives, on_device(): lax.all_to_all(result, 'frame', split_axis=0, concat_axis=0, tiled=True)  35.2 us
    all_to_all x1, waiting for transfers between devices, on_device(): lax.all_to_all(tokens, 'frame', split_axis=0, concat_axis=0, tiled=True)  30.6 us
    pallas_call x1, Pallas kernels, attention(): pl.pallas_call(attention_kernel, out_shape=jax.ShapeDtypeStruct(tokens.sh...  26.6 us
    pallas_call x1, Pallas kernels, strided(): pl.pallas_call(strided_kernel, out_shape=jax.ShapeDtypeStruct((half_rows,...  18.2 us
    pallas_call x1, Pallas kernels, temporal(): pl.pallas_call(temporal_kernel, out_shape=jax.ShapeDtypeStruct((rows, fra...  11.9 us
    ppermute x3, starting transfers between devices, passed_along(): lax.ppermute(value, axis, [(source, source + steps) for source in range(l...  8.81 us
  transfers between devices with their start and end apart: 5, of which 5 were waited for; matrix products, arithmetic and copies ran while one was open for 3% of the time, Pallas kernels for 4%

profile of v1, /device:TPU:0, one launch (start us, length us, event | category | flops | bytes accessed | tf_op | source)
XLA Modules:
  0.0 277.1 jit_solution(12031902519116612321)
XLA Ops:
  6.5 0.0 all-gather.2.cloned.1.call-start
  6.5 5.0 %copy.14 = bf16[3,3,640,160]{3,2,1,0:T(8,128)(2,1)} copy(bf16[3,3,640,160]{2,3,1,0:T(8,128)(2,1)} %param.14) | data formatting | bytes 3686400 | tf_op args[3]
  11.6 4.1 %shard_map.110 = bf16[40,5760]{1,0:T(8,128)(2,1)} custom-call(s32[1]{0:T(128)} %bitcast.1.index_ref, bf16[5760,160]{1,0:T(8,128)(2,1)} %bitcast.6), custom_call_target="tpu_custom_call" | custom-call | flops 73728000 | bytes 2304000 | tf_op jit(solution)/shard_map/pallas_call | solution.py:37
  15.7 0.0 all-gather.2.cloned.1.call-update
  15.7 0.0 copy-done
  15.7 0.0 copy-start.5
  15.8 0.2 fusion
  16.0 1.3 collective-permute-start.1
  17.3 5.6 %collective-permute-start = (bf16[1,16,64,640]{3,2,1,0:T(8,128)(2,1)S(1)}, bf16[1,16,64,640]{3,2,1,0:T(8,128)(2,1)S(1)}, u32[]{:S(2)}, u32[]{:S(2)}) collective-permute-start(bf16[1,16,64,640]{3,2,1,0:T(8,128)(2,1)S(1)} %get-tuple-element.5), channel_id=1, source_target_pairs={{0,4},{4,8},{8,12},{12,16},{16,20},{20,24},{24,28},{1,5},{5,9},{9,... | collective-permute-start | bytes 3932168 | tf_op jit(solution)/shard_map/ppermute | solution.py:18
  22.9 0.0 copy-done.5
  22.9 0.6 reshape.27.bias_ref
  23.5 29.5 %collective-permute-done.1 = bf16[1,16,64,640]{3,2,1,0:T(8,128)(2,1)S(1)} collective-permute-done((bf16[1,16,64,640]{3,2,1,0:T(8,128)(2,1)S(1)}, bf16[1,16,64,640]{3,2,1,0:T(8,128)(2,1)S(1)}, u32[]{:S(2)}, u32[]{:S(2)}) %collective-permute-start.1) | collective-permute-done | bytes 1310752 | tf_op jit(solution)/shard_map/ppermute | solution.py:18
  53.0 1.8 pad_maximum_fusion.1.after_ref
  54.7 33.0 %collective-permute-done = bf16[1,16,64,640]{3,2,1,0:T(8,128)(2,1)S(1)} collective-permute-done((bf16[1,16,64,640]{3,2,1,0:T(8,128)(2,1)S(1)}, bf16[1,16,64,640]{3,2,1,0:T(8,128)(2,1)S(1)}, u32[]{:S(2)}, u32[]{:S(2)}) %collective-permute-start) | collective-permute-done | bytes 1310752 | tf_op jit(solution)/shard_map/ppermute | solution.py:18
  87.8 1.8 pad_maximum_fusion.before_ref
  89.5 11.9 %shard_map.109 = bf16[16,2,32,1920]{3,2,1,0:T(8,128)(2,1)} custom-call(bf16[2,16,64,640]{3,2,1,0:T(8,128)(2,1)} %pad_maximum_fusion.before_ref, bf16[2,16,64,640]{3,2,1,0:T(8,128)(2,1)} %centre_ref.1, bf16[2,16,64,640]{3,2,1,0:T(8,128)(2,1)} %pad_maximum_fusion.1.after_ref, bf16[3,640,640]{2,1,0:T(8,128)(2,1)} %weight_ref.1, f32[1,640]{1,0:T(1,128)} %reshape.27.bias_ref), custom_call_target="tpu_custom_call" | custom-call | flops 5033164800 | bytes 11796480 | tf_op jit(solution)/shard_map/pallas_call | solution.py:80
  101.4 1.0 slice.14
  102.4 1.9 collective-permute-start.2
  104.3 0.0 copy-done.2
  104.3 0.6 reshape.31.bias_ref
  104.9 0.8 collective-permute-done.2.upper_ref
  105.8 46.4 %all-gather.2.cloned.1.call-done.weight_ref = bf16[1280,5760]{1,0:T(8,128)(2,1)} async-done(((bf16[40,5760]{1,0:T(8,128)(2,1)}), bf16[1280,5760]{1,0:T(8,128)(2,1)}) %all-gather.2.cloned.1.call-update) | async-done | bytes 14745616 | tf_op jit(solution)/shard_map/all_gather | solution.py:271
  152.2 0.0 copy-done.6
  152.2 18.2 %shard_map.111 = bf16[8,2,32,1280]{3,2,1,0:T(8,128)(2,1)} custom-call(bf16[8,2,2,32,1920]{4,3,2,1,0:T(8,128)(2,1)} %bitcast.10, bf16[1,2,32,1920]{3,2,1,0:T(8,128)(2,1)} %copy-done.6, bf16[1280,5760]{1,0:T(8,128)(2,1)} %all-gather.2.cloned.1.call-done.weight_ref, f32[1,1280]{1,0:T(1,128)} %reshape.31.bias_ref), custom_call_target="tpu_custom_call" | custom-call | flops 7549747200 | bytes 19988480 | tf_op jit(solution)/shard_map/pallas_call | solution.py:136
  170.4 4.0 %all-to-all-start = ((bf16[8,2,32,1280]{3,2,1,0:T(8,128)(2,1)}), bf16[8,2,32,1280]{3,2,1,0:T(8,128)(2,1)S(1)}, u32[]{:S(2)}, u32[]{:S(2)}) async-start(bf16[8,2,32,1280]{3,2,1,0:T(8,128)(2,1)} %shard_map.111), calls=%async_computation | async-start | bytes 2621440 | tf_op jit(solution)/shard_map/all_to_all | solution.py:288
  174.4 0.6 reshape.33.gain_ref
  175.0 0.6 reshape.34.bias_ref
  175.6 30.6 %all-to-all-done = bf16[8,2,32,1280]{3,2,1,0:T(8,128)(2,1)S(1)} async-done(((bf16[8,2,32,1280]{3,2,1,0:T(8,128)(2,1)}), bf16[8,2,32,1280]{3,2,1,0:T(8,128)(2,1)S(1)}, u32[]{:S(2)}, u32[]{:S(2)}) %all-to-all-start) | async-done | bytes 1310752 | tf_op jit(solution)/shard_map/all_to_all | solution.py:288
  206.2 1.1 copy-done.1
  207.3 26.6 %shard_map.112 = bf16[16,32,1280]{2,1,0:T(8,128)(2,1)} custom-call(bf16[16,32,1280]{2,1,0:T(8,128)(2,1)} %bitcast.8, f32[1,1280]{1,0:T(1,128)} %reshape.33.gain_ref, f32[1,1280]{1,0:T(1,128)} %reshape.34.bias_ref, bf16[1280,1280]{1,0:T(8,128)(2,1)} %wq_hbm.1, bf16[1280,1280]{1,0:T(8,128)(2,1)} %wk_hbm.1, bf16[1280,1280]{1,0:T(8,128)(2,1)} %wv_hbm.1, ...), custom_call_target="tpu_custom_call" | custom-call | flops 6710886400 | bytes 15728640 | tf_op jit(solution)/shard_map/pallas_call | solution.py:237
  233.9 35.2 %all_to_all.10 = bf16[8,2,32,1280]{3,2,1,0:T(8,128)(2,1)S(1)} all-to-all(bf16[8,2,32,1280]{3,2,1,0:T(8,128)(2,1)} %bitcast.9), channel_id=1, replica_groups=mesh['frame'=8,'row'=4] {'frame'}, dimensions={0} | all-to-all | bytes 2621440 | tf_op jit(solution)/shard_map/all_to_all | solution.py:292
  269.1 1.1 copy.15
  (8 shorter events, 0.0 us)
Async XLA Ops:
  6.5 145.6 %all-gather.2.cloned.1.call-start = ((), (), s32[]{:S(2)}) async-start(), calls=%async_computation.2 | async-start | bytes 15206400 | tf_op jit(solution)/shard_map/all_gather | solution.py:271
  11.6 4.2 %copy-start = (bf16[2,16,64,640]{3,2,1,0:T(8,128)(2,1)S(1)}, bf16[2,16,64,640]{3,2,1,0:T(8,128)(2,1)}, u32[]{:S(2)}) copy-start(bf16[2,16,64,640]{3,2,1,0:T(8,128)(2,1)} %centre_ref.1) | copy-start | bytes 7864324
  15.7 7.2 %copy-start.5 = (f32[640]{0:T(1024)S(1)}, f32[640]{0:T(1024)}, u32[]{:S(2)}) copy-start(f32[640]{0:T(1024)} %param.13) | copy-start | bytes 7684
  16.0 37.0 %collective-permute-start.1 = (bf16[1,16,64,640]{3,2,1,0:T(8,128)(2,1)S(1)}, bf16[1,16,64,640]{3,2,1,0:T(8,128)(2,1)S(1)}, u32[]{:S(2)}, u32[]{:S(2)}) collective-permute-start(bf16[1,16,64,640]{3,2,1,0:T(8,128)(2,1)S(1)} %get-tuple-element.6), channel_id=1, source_target_pairs={{4,0},{8,4},{12,8},{16,12},{20,16},{24,20},{28,24},{5,1},{9,5},{13... | collective-permute-start | bytes 3932168 | tf_op jit(solution)/shard_map/ppermute | solution.py:18
  17.3 70.5 %collective-permute-start = (bf16[1,16,64,640]{3,2,1,0:T(8,128)(2,1)S(1)}, bf16[1,16,64,640]{3,2,1,0:T(8,128)(2,1)S(1)}, u32[]{:S(2)}, u32[]{:S(2)}) collective-permute-start(bf16[1,16,64,640]{3,2,1,0:T(8,128)(2,1)S(1)} %get-tuple-element.5), channel_id=1, source_target_pairs={{0,4},{4,8},{8,12},{12,16},{16,20},{20,24},{24,28},{1,5},{5,9},{9,... | collective-permute-start | bytes 3932168 | tf_op jit(solution)/shard_map/ppermute | solution.py:18
  89.5 14.8 %copy-start.2 = (f32[1280]{0:T(1024)S(1)}, f32[1280]{0:T(1024)}, u32[]{:S(2)}) copy-start(f32[1280]{0:T(1024)} %param.15) | copy-start | bytes 15364
  102.4 3.4 %collective-permute-start.2 = (bf16[1,2,32,1920]{3,2,1,0:T(8,128)(2,1)S(1)}, bf16[1,2,32,1920]{3,2,1,0:T(8,128)(2,1)S(1)}, u32[]{:S(2)}, u32[]{:S(2)}) collective-permute-start(bf16[1,2,32,1920]{3,2,1,0:T(8,128)(2,1)S(1)} %slice.14), channel_id=1, source_target_pairs={{0,1},{1,2},{2,3},{4,5},{5,6},{6,7},{8,9},{9,10},{10,11},{12,13},{... | collective-permute-start | bytes 737288 | tf_op jit(solution)/shard_map/ppermute | solution.py:18
  105.8 46.4 %copy-start.6 = (bf16[1,2,32,1920]{3,2,1,0:T(8,128)(2,1)}, bf16[1,2,32,1920]{3,2,1,0:T(8,128)(2,1)S(1)}, u32[]{:S(2)}) copy-start(bf16[1,2,32,1920]{3,2,1,0:T(8,128)(2,1)S(1)} %collective-permute-done.2.upper_ref) | copy-start | bytes 737284
  170.4 4.0 %copy-start.3 = (f32[1280]{0:T(1024)S(1)}, f32[1280]{0:T(1024)}, u32[]{:S(2)}) copy-start(f32[1280]{0:T(1024)} %param.16) | copy-start | bytes 15364
  170.4 4.6 %copy-start.4 = (f32[1280]{0:T(1024)S(1)}, f32[1280]{0:T(1024)}, u32[]{:S(2)}) copy-start(f32[1280]{0:T(1024)} %param.21) | copy-start | bytes 15364
  170.4 35.8 %all-to-all-start = ((bf16[8,2,32,1280]{3,2,1,0:T(8,128)(2,1)}), bf16[8,2,32,1280]{3,2,1,0:T(8,128)(2,1)S(1)}, u32[]{:S(2)}, u32[]{:S(2)}) async-start(bf16[8,2,32,1280]{3,2,1,0:T(8,128)(2,1)} %shard_map.111), calls=%async_computation | async-start | bytes 2621440 | tf_op jit(solution)/shard_map/all_to_all | solution.py:288
  206.2 1.1 copy-start.1
Sparse Core Ops, SparseCore 0:
  15.9 136.2 all-gather.1
